TPU v7x, 512 devices: a whole 4x8x8 slice. The times are simulated.
512 devices in a mesh: grp: 16 (over x_hi, y), sub: 32 (over z, x_lo, core).
Axes of the slice: x: 4 (x_hi: 2, x_lo: 2; x = x_hi * 2 + x_lo), y: 8, z: 8, core: 2. Of those that a mesh axis runs over, the one named last changes fastest.
Arguments:
- control: float32 [16, 32, 384, 768], P('grp', None, 'sub'), may hold values from -6 to 6
- perturbation: float32 [16, 32, 384, 768], P('grp', None, 'sub'), may hold values from -6 to 6
- weight: float32 [32, 384, 768], P('grp', 'sub'), may hold values from 0.25 to 2
- half_width: int32 [384], replicated, may hold values from 1 to 12, as said below
Outputs:
- increment: float32 [32, 384, 768], P('grp', 'sub')
- adjoint: float32 [16, 32, 384, 768], P('grp', None, 'sub')
Inputs may be any that keep to these rules, and one draw needn't show every extreme that they name: `half_width`: at least one latitude has half-width 12.
All inputs are finite; a program needn't handle non-finite values.
Results may differ from a plain program's by a relative error of at most 0.0001.
Values sent between devices are 32-bit elements; how exact they have to be, the bound alone decides.
A program may use at most 64 MiB of HBM per device.

v0:
```python
import jax
import jax.numpy as jnp
from jax import lax
from jax.sharding import PartitionSpec as P

lon_sigma = 4.0
lon_reach = 12.0


def lat_matrix(half_width):
    length = half_width.shape[0]
    row_index = jnp.arange(length, dtype=jnp.int32)[:, None]
    col_index = jnp.arange(length, dtype=jnp.int32)[None, :]
    offset = (row_index - col_index).astype(jnp.float32)
    reach_rows = half_width.astype(jnp.float32)[:, None]
    spread_width = 0.5 * reach_rows + 0.5
    inside = jnp.abs(offset) <= reach_rows
    kernel = jnp.where(inside, jnp.exp(-0.5 * (offset / spread_width) ** 2), jnp.zeros_like(offset))
    return kernel / jnp.sum(kernel, axis=1, keepdims=True)


def lon_matrix(length):
    row_index = jnp.arange(length, dtype=jnp.int32)[:, None]
    col_index = jnp.arange(length, dtype=jnp.int32)[None, :]
    offset = (row_index - col_index) % length
    offset = jnp.where(offset * 2 > length, offset - length, offset).astype(jnp.float32)
    inside = jnp.abs(offset) <= lon_reach
    kernel = jnp.where(inside, jnp.exp(-0.5 * (offset / lon_sigma) ** 2), jnp.zeros_like(offset))
    return kernel / jnp.sum(kernel, axis=1, keepdims=True)


def along_lon(values, lon_right):
    flattened = values.reshape(-1, values.shape[-1])
    mixed = jnp.dot(
        flattened, lon_right, precision=lax.Precision.HIGHEST, preferred_element_type=jnp.float32
    )
    return mixed.reshape(values.shape)


def level_apply(values, lat_left, lon_right):
    flattened = values.reshape(-1, values.shape[2], values.shape[3])
    halfway = jnp.einsum("ij,ljk->lik", lat_left, flattened, precision=lax.Precision.HIGHEST)
    return along_lon(halfway, lon_right).reshape(values.shape)


def regroup_filter(values, lat_left, lon_right):
    filtered = level_apply(
        lax.all_to_all(values, "sub", split_axis=1, concat_axis=2, tiled=True), lat_left, lon_right
    )
    return lax.all_to_all(filtered, "sub", split_axis=2, concat_axis=1, tiled=True)


def shards(control, perturbation, weight, half_width):
    lat_filter = lat_matrix(half_width)
    lon_filter = lon_matrix(control.shape[3])
    filtered = regroup_filter(control, lat_filter, lon_filter.T)
    partial_sum = jnp.sum(perturbation * filtered, axis=0)
    level_share = weight.shape[0]
    summed = lax.psum(partial_sum, "grp")
    weight_full = lax.all_gather(weight, "grp", axis=0, tiled=True)
    weighted = weight_full * summed
    increment = lax.dynamic_slice_in_dim(
        weighted, lax.axis_index("grp") * level_share, level_share, 0
    )
    products = perturbation * weighted[None]
    adjoint = regroup_filter(products, lat_filter.T, lon_filter)
    return (increment, adjoint)


def solution(mesh):
    return jax.shard_map(
        shards,
        mesh=mesh,
        in_specs=(
            P("grp", None, "sub", None),
            P("grp", None, "sub", None),
            P("grp", "sub", None),
            P(),
        ),
        out_specs=(P("grp", "sub", None), P("grp", None, "sub", None)),
        check_vma=False,
    )
```

profile of v0, /device:TPU:3, one launch (start us, length us, event | category | flops | bytes accessed | tf_op | source)
XLA Modules:
  0.0 436.1 jit_solution(14705779404867223133)
XLA Ops:
  7.2 3.1 copy.47
  10.3 12.3 %all-to-all-start = ((f32[1,32,12,768]{3,2,0,1:T(8,128)}), f32[1,32,12,768]{3,2,0,1:T(8,128)S(1)}, u32[]{:S(2)}, u32[]{:S(2)}) async-start(f32[1,32,12,768]{3,2,0,1:T(8,128)} %copy.47), calls=%async_computation | async-start | bytes 3145728 | tf_op jit(solution)/shard_map/all_to_all | solution.py:48
  23.1 2.6 fusion.5
  25.7 36.0 %all-to-all-done = f32[1,32,12,768]{3,2,0,1:T(8,128)S(1)} async-done(((f32[1,32,12,768]{3,2,0,1:T(8,128)}), f32[1,32,12,768]{3,2,0,1:T(8,128)S(1)}, u32[]{:S(2)}, u32[]{:S(2)}) %all-to-all-start) | async-done | bytes 1179680 | tf_op jit(solution)/shard_map/all_to_all | solution.py:48
  61.9 2.3 fusion.7
  64.2 6.2 %convolution_bitcast_fusion.2 = f32[1,1,384,768]{3,2,1,0:T(8,128)S(1)} fusion(f32[384,768]{1,0:T(8,128)S(1)} %fusion.7, f32[768]{0:T(1024)S(1)} %fusion.5), kind=kOutput, calls=%fused_computation.12 | convolution fusion | flops 2729115648 | bytes 2362368 | tf_op jit(solution)/shard_map/dot_general | solution.py:34
  70.4 2.2 copy.48
  72.6 4.7 %all-to-all-start.1 = ((f32[1,1,384,768]{3,1,0,2:T(1,128)}), f32[1,1,384,768]{3,1,0,2:T(1,128)S(1)}, u32[]{:S(2)}, u32[]{:S(2)}) async-start(f32[1,1,384,768]{3,1,0,2:T(1,128)} %copy.48), calls=%async_computation.1 | async-start | bytes 2359296 | tf_op jit(solution)/shard_map/all_to_all | solution.py:50
  77.4 0.6 copy.46
  78.1 30.2 %all-to-all-done.1 = f32[1,1,384,768]{3,1,0,2:T(1,128)S(1)} async-done(((f32[1,1,384,768]{3,1,0,2:T(1,128)}), f32[1,1,384,768]{3,1,0,2:T(1,128)S(1)}, u32[]{:S(2)}, u32[]{:S(2)}) %all-to-all-start.1) | async-done | bytes 1179680 | tf_op jit(solution)/shard_map/all_to_all | solution.py:50
  108.2 1.3 fusion.4
  109.5 55.0 %all-gather.2.cloned.1.call-done = f32[32,12,768]{2,1,0:T(8,128)} async-done(((f32[2,12,768]{2,1,0:T(8,128)}), f32[32,12,768]{2,1,0:T(8,128)}) %all-gather.2.cloned.1.call-update) | async-done | bytes 1179664 | tf_op jit(solution)/shard_map/all_gather | solution.py:60
  164.6 158.1 %all-reduce.2.cloned.1.call-done = f32[32,12,768]{2,0,1:T(8,128)} async-done(((f32[32,12,768]{2,0,1:T(8,128)}), f32[32,12,768]{2,0,1:T(8,128)}) %all-reduce.2.cloned.1.call-update) | async-done | bytes 1179664 | tf_op jit(solution)/shard_map/psum | solution.py:59
  322.6 3.6 bitcast_multiply_fusion
  326.2 1.2 copy.51
  327.4 51.3 %all_to_all.42 = f32[1,32,12,768]{3,0,2,1:T(1,128)S(1)} all-to-all(f32[1,32,12,768]{3,0,2,1:T(1,128)S(1)} %copy.51), channel_id=1, replica_groups=mesh['grp'=16,'sub'=32] {'sub'}, dimensions={1} | all-to-all | bytes 2359296 | tf_op jit(solution)/shard_map/all_to_all | solution.py:48
  378.7 2.8 reduce
  381.7 2.7 convolution_bitcast_fusion.1
  384.3 5.2 %convolution_bitcast_fusion = f32[1,1,384,768]{3,2,1,0:T(8,128)S(1)} fusion(f32[384,768]{0,1:T(8,128)S(1)} %convolution_bitcast_fusion.1, f32[768]{0:T(1024)S(1)} %fusion.5), kind=kOutput, calls=%fused_computation.10 | convolution fusion | flops 2729115648 | bytes 2362368 | tf_op jit(solution)/shard_map/dot_general | solution.py:34
  389.5 2.2 copy.52
  391.8 4.5 %all-to-all-start.3 = ((f32[1,1,384,768]{3,1,0,2:T(1,128)}), f32[1,1,384,768]{3,1,0,2:T(1,128)S(1)}, u32[]{:S(2)}, u32[]{:S(2)}) async-start(f32[1,1,384,768]{3,1,0,2:T(1,128)} %copy.52), calls=%async_computation.3 | async-start | bytes 2359296 | tf_op jit(solution)/shard_map/all_to_all | solution.py:50
  396.3 1.6 constant_dynamic-slice_fusion
  397.9 30.1 %all-to-all-done.3 = f32[1,1,384,768]{3,1,0,2:T(1,128)S(1)} async-done(((f32[1,1,384,768]{3,1,0,2:T(1,128)}), f32[1,1,384,768]{3,1,0,2:T(1,128)S(1)}, u32[]{:S(2)}, u32[]{:S(2)}) %all-to-all-start.3) | async-done | bytes 1179680 | tf_op jit(solution)/shard_map/all_to_all | solution.py:50
  428.1 1.2 copy.53
  (15 shorter events, 0.8 us)
Async XLA Ops:
  10.3 12.4 %copy-start.2 = (s32[384]{0:T(512)S(1)}, s32[384]{0:T(512)}, u32[]{:S(2)}) copy-start(s32[384]{0:T(512)} %param.7) | copy-start | bytes 4612
  10.3 51.4 %all-to-all-start = ((f32[1,32,12,768]{3,2,0,1:T(8,128)}), f32[1,32,12,768]{3,2,0,1:T(8,128)S(1)}, u32[]{:S(2)}, u32[]{:S(2)}) async-start(f32[1,32,12,768]{3,2,0,1:T(8,128)} %copy.47), calls=%async_computation | async-start | bytes 3145728 | tf_op jit(solution)/shard_map/all_to_all | solution.py:48
  72.6 4.8 %copy-start.1 = (f32[2,12,768]{2,0,1:T(2,128)S(1)}, f32[2,12,768]{2,0,1:T(2,128)}, u32[]{:S(2)}) copy-start(f32[2,12,768]{2,0,1:T(2,128)} %param.6) | copy-start | bytes 221188
  72.6 35.7 %copy-start = (f32[1,32,12,768]{3,1,2,0:T(8,128)S(1)}, f32[1,32,12,768]{3,1,2,0:T(8,128)}, u32[]{:S(2)}) copy-start(f32[1,32,12,768]{3,1,2,0:T(8,128)} %param.5) | copy-start | bytes 3538948
  72.6 35.7 %all-to-all-start.1 = ((f32[1,1,384,768]{3,1,0,2:T(1,128)}), f32[1,1,384,768]{3,1,0,2:T(1,128)S(1)}, u32[]{:S(2)}, u32[]{:S(2)}) async-start(f32[1,1,384,768]{3,1,0,2:T(1,128)} %copy.48), calls=%async_computation.1 | async-start | bytes 2359296 | tf_op jit(solution)/shard_map/all_to_all | solution.py:50
  77.3 87.3 %all-gather.2.cloned.1.call-start = ((), (), s32[]{:S(2)}) async-start(), calls=%async_computation.4 | async-start | bytes 1671168 | tf_op jit(solution)/shard_map/all_gather | solution.py:60
  78.0 244.6 %all-reduce.2.cloned.1.call-start = ((), (), s32[]{:S(2)}) async-start(), calls=%async_computation.5 | async-start | bytes 2359296 | tf_op jit(solution)/shard_map/psum | solution.py:59
  391.8 36.3 %all-to-all-start.3 = ((f32[1,1,384,768]{3,1,0,2:T(1,128)}), f32[1,1,384,768]{3,1,0,2:T(1,128)S(1)}, u32[]{:S(2)}, u32[]{:S(2)}) async-start(f32[1,1,384,768]{3,1,0,2:T(1,128)} %copy.52), calls=%async_computation.3 | async-start | bytes 2359296 | tf_op jit(solution)/shard_map/all_to_all | solution.py:50
Sparse Core Ops, SparseCore 0:
  81.3 83.2 all-gather.1
  168.1 154.5 all-reduce.1
where the time goes:
time: 437 us; the launch traced here: 436 us
  waiting for transfers between devices  309 us (71%)
  blocking collectives  51.3 us (12%)
  starting transfers between devices  21.7 us (5%)
  matrix products  16.3 us (4%)
  between operations  14.2 us (3%)
  local copies, waits for them, and re-layouts  12.6 us (3%)
  other arithmetic  10.7 us (2%)
    psum x1, waiting for transfers between devices, shards(): summed = lax.psum(partial_sum, 'grp')  158 us
    all_to_all x2, waiting for transfers between devices, regroup_filter(): lax.all_to_all(filtered, 'sub', split_axis=2, concat_axis=1, tiled=True)  60.3 us
    all_gather x1, waiting for transfers between devices, shards(): weight_full = lax.all_gather(weight, 'grp', axis=0, tiled=True)  55 us
    all_to_all x1, blocking collectives, regroup_filter(): lax.all_to_all(values, 'sub', split_axis=1, concat_axis=2, tiled=True)  51.3 us
    all_to_all x1, waiting for transfers between devices, regroup_filter(): lax.all_to_all(values, 'sub', split_axis=1, concat_axis=2, tiled=True)  36 us
    all_to_all x1, starting transfers between devices, regroup_filter(): lax.all_to_all(values, 'sub', split_axis=1, concat_axis=2, tiled=True)  12.3 us
    dot_general x2, matrix products, along_lon(): jnp.dot(flattened, lon_right, precision=lax.Precision.HIGHEST, preferred_...  11.4 us
    all_to_all x2, starting transfers between devices, regroup_filter(): lax.all_to_all(filtered, 'sub', split_axis=2, concat_axis=1, tiled=True)  9.25 us
  transfers between devices with their start and end apart: 5, of which 5 were waited for; matrix products, arithmetic and copies ran while one was open for 1% of the time, Pallas kernels for 0%

commit v1 on v0

v1 whole, which is shorter than its diff:
```python
import functools
import math

import jax
import jax.numpy as jnp
from jax import lax
from jax.experimental import pallas as pl
from jax.experimental.pallas import tpu as pltpu
from jax.sharding import PartitionSpec as P

MESH = pl.DeviceIdType.MESH
ROWS = 12
TILE = 8
CHUNKS = 4
LON = 768
HALF = 384
RING = 8
TAPS = 2 * ROWS + 1
PAD = 12
REACH = 12
LON_SUM = sum(math.exp(-0.5 * (d / 4.0) ** 2) for d in range(-REACH, REACH + 1))
WINDOW = 512
OUT = 256


def kernel(
    n_sub,
    hw,
    control,
    pert,
    weight,
    inc_out,
    adj_out,
    cbuf,
    pbuf,
    ybuf,
    lhs_hi,
    lhs_lo,
    f_hi,
    f_lo,
    wtab,
    prod,
    rs_f,
    rs_b,
    tot,
    xin,
    wpart,
    wbuf,
    wfull,
    inc,
    own,
    to_l,
    to_r,
    from_l,
    from_r,
    incst,
    c_send,
    c_recv,
    load_sem,
    rsf_send,
    rsf_recv,
    rsb_send,
    rsb_recv,
    x_send,
    x_recv,
    ag_send,
    ag_recv,
    a_send,
    a_recv,
    w_send,
    w_recv,
    out_sem,
):
    g = lax.axis_index("grp")
    s = lax.axis_index("sub")
    y = lax.rem(g, RING)
    xh = lax.div(g, RING)
    base = xh * RING
    core = lax.rem(s, 2)
    sign = 1 - 2 * core
    left = lax.rem(s + n_sub - 1, n_sub)
    right = lax.rem(s + 1, n_sub)

    def ring(offset):
        return lax.rem(y + sign * offset + RING, RING)

    ahead = base + ring(1)
    behind = base + ring(-1)
    partner = (1 - xh) * RING + y

    def remote(src, dst, ss, rs, grp, sub):
        return pltpu.make_async_remote_copy(
            src_ref=src, dst_ref=dst, send_sem=ss, recv_sem=rs, device_id=(grp, sub), device_id_type=MESH
        )

    pending = []

    def launch(copy):
        copy.start()
        pending.append(copy)
        return copy

    loads = {}
    for k in range(CHUNKS):
        levels = pl.ds(k * TILE, TILE)
        loads["c", k] = pltpu.make_async_copy(control.at[:, levels, :], cbuf.at[k, pl.ds(ROWS, ROWS)], load_sem.at[0, k])
        loads["p", k] = pltpu.make_async_copy(pert.at[:, levels, :], pbuf.at[k], load_sem.at[1, k])
        loads["c", k].start()
        loads["p", k].start()

    def weight_piece(ref, owner):
        rows = pl.ds(3 * lax.div(owner, 2), 3)
        cols = pl.ds(pl.multiple_of(lax.rem(owner, 2) * HALF, 128), HALF)
        return ref.at[rows, :, cols]

    loads["w"] = pltpu.make_async_copy(weight_piece(weight, y), wbuf.at[g], load_sem.at[2, 0])
    loads["w"].start()

    barrier = pltpu.get_barrier_semaphore()
    for grp, sub in ((g, left), (g, right), (ahead, s), (behind, s), (partner, s)):
        pl.semaphore_signal(barrier, inc=1, device_id=(grp, sub), device_id_type=MESH)
    pl.semaphore_wait(barrier, 5)

    halos = {}

    def send_control(k):
        src = control.at[:, pl.ds(k * TILE, TILE), :]
        halos["c", k] = (
            launch(remote(src, cbuf.at[k, pl.ds(0, ROWS)], c_send.at[k, 0], c_recv.at[k, 0], g, right)),
            launch(remote(src, cbuf.at[k, pl.ds(2 * ROWS, ROWS)], c_send.at[k, 1], c_recv.at[k, 1], g, left)),
        )

    send_control(0)
    send_control(1)
    halos["w"] = launch(remote(weight, wpart, w_send.at[0], w_recv.at[0], partner, s))

    def fill(r, carry):
        row = s * ROWS + r
        reach = jnp.full((8, 128), hw[row].astype(jnp.float32))
        spread = 0.5 * reach + 0.5
        values = []
        for d in range(ROWS + 1):
            e = jnp.exp(-0.5 * (d / spread) ** 2)
            values.append(jnp.where(d <= reach, e, 0.0))
        at = jnp.full((8, 128), row)
        parts = {}
        total = values[0]
        parts[0] = values[0]
        for d in range(1, ROWS + 1):
            parts[-d] = jnp.where(at - d >= 0, values[d], 0.0)
            parts[d] = jnp.where(at + d < n_sub * ROWS, values[d], 0.0)
            total = total + parts[-d] + parts[d]
        zero = jnp.zeros((8, 128), jnp.float32)
        for i in range(PAD):
            wtab[r, i] = zero
            wtab[r, PAD + TAPS + i] = zero
        for d in range(-ROWS, ROWS + 1):
            wtab[r, PAD + ROWS + d] = parts[d] / total
        return carry

    lax.fori_loop(0, ROWS, fill, 0)

    def fill_lon(i, carry):
        start = pl.multiple_of(i * 64, 64)
        a = lax.broadcasted_iota(jnp.int32, (64, OUT), 0) + i * 64
        b = lax.broadcasted_iota(jnp.int32, (64, OUT), 1)
        d = (a - 128 - b).astype(jnp.float32)
        f = jnp.where(jnp.abs(d) <= REACH, jnp.exp(-0.5 * (d / 4.0) ** 2) / LON_SUM, 0.0)
        hi = f.astype(jnp.bfloat16)
        f_hi[pl.ds(start, 64), :] = hi
        f_lo[pl.ds(start, 64), :] = (f - hi.astype(jnp.float32)).astype(jnp.bfloat16)
        return carry

    lax.fori_loop(0, WINDOW // 64, fill_lon, 0)

    count = ROWS * TILE

    def lon_filter():
        for t in range(3):
            for i in range(4):
                c = (256 * t - 128 + 128 * i) % LON
                v = ybuf[:, c : c + 128]
                hi = v.astype(jnp.bfloat16)
                lhs_hi[count * t : count * (t + 1), 128 * i : 128 * (i + 1)] = hi
                lhs_lo[count * t : count * (t + 1), 128 * i : 128 * (i + 1)] = (v - hi.astype(jnp.float32)).astype(
                    jnp.bfloat16
                )
        h = lhs_hi[...]
        fh = f_hi[...]
        res = jnp.dot(h, fh, preferred_element_type=jnp.float32)
        res += jnp.dot(h, f_lo[...], preferred_element_type=jnp.float32)
        res += jnp.dot(lhs_lo[...], fh, preferred_element_type=jnp.float32)
        for t in range(3):
            ybuf[:, OUT * t : OUT * (t + 1)] = res[count * t : count * (t + 1)]

    def wide(w):
        return jnp.concatenate([w] * 6, axis=1)

    def piece_slices(o):
        return 3 * (o // 2), HALF * (o % 2)

    def forward(k):
        loads["c", k].wait()
        loads["p", k].wait()
        for copy in halos["c", k]:
            copy.wait_recv()

        def row(r, carry):
            acc = wide(wtab[r, PAD]) * cbuf[k, r]
            for d in range(1, TAPS):
                acc = acc + wide(wtab[r, PAD + d]) * cbuf[k, r + d]
            ybuf[pl.ds(pl.multiple_of(r * TILE, TILE), TILE), :] = acc
            return carry

        lax.fori_loop(0, ROWS, row, 0)
        lon_filter()
        for o in range(RING):
            r0, c0 = piece_slices(o)
            part = ybuf[r0 * TILE : (r0 + 3) * TILE, c0 : c0 + HALF].reshape(3, TILE, HALF)
            prod[k, o] = part * pbuf[k, r0 : r0 + 3, :, c0 : c0 + HALF]

    f_copies, b_copies = {}, {}

    def send_f(k, t):
        src = prod.at[k, ring(4)] if t == 0 else rs_f.at[k, t - 1]
        f_copies[k, t] = launch(remote(src, rs_f.at[k, t], rsf_send.at[k, t], rsf_recv.at[k, t], ahead, s))

    def send_b(k, t):
        src = prod.at[k, ring(-3)] if t == 0 else rs_b.at[k, t - 1]
        b_copies[k, t] = launch(remote(src, rs_b.at[k, t], rsb_send.at[k, t], rsb_recv.at[k, t], behind, s))

    def stage0(k):
        forward(k)
        send_f(k, 0)
        send_b(k, 0)

    def reduce_step(k, t):
        f_copies[k, t].wait_recv()
        rs_f[k, t] = rs_f[k, t] + prod[k, ring(3 - t)]
        send_f(k, t + 1)
        if t < 2:
            b_copies[k, t].wait_recv()
            rs_b[k, t] = rs_b[k, t] + prod[k, ring(t - 2)]
            send_b(k, t + 1)

    def stage4(k):
        f_copies[k, 3].wait_recv()
        b_copies[k, 2].wait_recv()
        tot[k] = prod[k, y] + rs_f[k, 3] + rs_b[k, 2]
        halos["x", k] = launch(remote(tot.at[k], xin.at[k], x_send.at[k], x_recv.at[k], partner, s))

    weights = []

    def send_weights():
        halos["w"].wait_recv()
        for j in range(1, RING):
            dest = lax.rem(y + j, RING)
            for i, (ref, owner) in enumerate(((weight, g), (wpart, partner))):
                n = 2 * j + i
                weights.append(
                    launch(
                        remote(weight_piece(ref, dest), wbuf.at[owner], w_send.at[n], w_recv.at[n], base + dest, s)
                    )
                )
        loads["x"] = pltpu.make_async_copy(weight_piece(wpart, y), wbuf.at[partner], load_sem.at[2, 1])
        loads["x"].start()

    def take_weights():
        loads["w"].wait()
        loads["x"].wait()
        for copy in weights:
            copy.wait_recv()
        for i in range(2 * RING):
            wfull[i // 4, :, 2 * (i % 4) : 2 * (i % 4) + 2, :] = wbuf[i]

    def stage5(k):
        halos["x", k].wait_recv()
        inc[k, y] = wfull[k] * (tot[k] + xin[k])
        halos["g", k] = []
        for j in (4, 3, -3, 2, -2, 1, -1):
            i = len(halos["g", k])
            halos["g", k].append(
                launch(remote(inc.at[k, y], inc.at[k, y], ag_send.at[k, i], ag_recv.at[k, i], base + ring(j), s))
            )

    def stage6(k):
        for copy in halos["g", k]:
            copy.wait_recv()
        for o in range(RING):
            r0, c0 = piece_slices(o)
            p = inc[k, o] * pbuf[k, r0 : r0 + 3, :, c0 : c0 + HALF]
            ybuf[r0 * TILE : (r0 + 3) * TILE, c0 : c0 + HALF] = p.reshape(3 * TILE, HALF)
        lon_filter()

        def row(j, carry):
            zero = jnp.zeros((TILE, LON), jnp.float32)
            mine, lo, hi = zero, zero, zero
            for i in range(ROWS):
                p = ybuf[i * TILE : (i + 1) * TILE, :]
                lo = lo + wide(wtab[i, PAD + j - i]) * p
                mine = mine + wide(wtab[i, PAD + ROWS + j - i]) * p
                hi = hi + wide(wtab[i, PAD + 2 * ROWS + j - i]) * p
            to_l[k, j] = lo
            own[k, j] = mine
            to_r[k, j] = hi
            return carry

        lax.fori_loop(0, ROWS, row, 0)
        halos["a", k] = (
            launch(remote(to_r.at[k], from_l.at[k], a_send.at[k, 0], a_recv.at[k, 0], g, right)),
            launch(remote(to_l.at[k], from_r.at[k], a_send.at[k, 1], a_recv.at[k, 1], g, left)),
        )

    outs = []

    def stage7(k):
        for copy in halos["a", k]:
            copy.wait_recv()

        def row(r, carry):
            own[k, r] = own[k, r] + from_l[k, r] + from_r[k, r]
            return carry

        lax.fori_loop(0, ROWS, row, 0)
        copy = pltpu.make_async_copy(own.at[k], adj_out.at[:, pl.ds(k * TILE, TILE), :], out_sem.at[k])
        copy.start()
        outs.append(copy)

    def write_increment():
        chunk = lax.div(g, 4)
        j = jnp.full((3, 2, HALF), lax.rem(g, 4))
        for o in range(RING):
            r0, c0 = piece_slices(o)
            v = inc[chunk, o]
            part = v[:, 6:8]
            for i in (2, 1, 0):
                part = jnp.where(j == i, v[:, 2 * i : 2 * i + 2], part)
            incst[r0 : r0 + 3, :, c0 : c0 + HALF] = part
        copy = pltpu.make_async_copy(incst, inc_out, out_sem.at[CHUNKS])
        copy.start()
        outs.append(copy)

    events = []
    for k in range(CHUNKS):
        t = 8.5 + 6.5 * k
        events.append((t, functools.partial(stage0, k)))
        for i in range(3):
            t += 2.2
            events.append((t, functools.partial(reduce_step, k, i)))
        t += 2.2
        events.append((t, functools.partial(stage4, k)))
        t += 3.5
        if k == 0:
            events.append((t - 0.2, take_weights))
        events.append((t, functools.partial(stage5, k)))
        t += 8.0
        events.append((t, functools.partial(stage6, k)))
        t += 9.0
        events.append((t, functools.partial(stage7, k)))
    events.append((8.6, functools.partial(send_control, 2)))
    events.append((17.4, functools.partial(send_control, 3)))
    events.append((15.2, send_weights))
    last6 = 8.5 + 6.5 * (CHUNKS - 1) + 8.8 + 3.5 + 8.0
    events.append((last6 + 0.1, write_increment))
    for _, event in sorted(events, key=lambda e: e[0]):
        event()

    for copy in pending:
        copy.wait_send()
    for copy in outs:
        copy.wait()


def shards(n_sub, control, perturbation, weight, half_width):
    f32 = jnp.float32
    vmem = lambda *shape: pltpu.VMEM(shape, f32)
    dma = pltpu.SemaphoreType.DMA
    hbm = pl.BlockSpec(memory_space=pl.ANY)
    increment, adjoint = pl.pallas_call(
        functools.partial(kernel, n_sub),
        out_shape=(
            jax.ShapeDtypeStruct((ROWS, 2, LON), f32),
            jax.ShapeDtypeStruct((ROWS, CHUNKS * TILE, LON), f32),
        ),
        in_specs=[pl.BlockSpec(memory_space=pltpu.SMEM), hbm, hbm, hbm],
        out_specs=(hbm, hbm),
        scratch_shapes=[
            vmem(CHUNKS, 3 * ROWS, TILE, LON),
            vmem(CHUNKS, ROWS, TILE, LON),
            vmem(ROWS * TILE, LON),
            pltpu.VMEM((3 * ROWS * TILE, WINDOW), jnp.bfloat16),
            pltpu.VMEM((3 * ROWS * TILE, WINDOW), jnp.bfloat16),
            pltpu.VMEM((WINDOW, OUT), jnp.bfloat16),
            pltpu.VMEM((WINDOW, OUT), jnp.bfloat16),
            vmem(ROWS, 2 * PAD + TAPS, 8, 128),
            vmem(CHUNKS, RING, 3, TILE, HALF),
            vmem(CHUNKS, 4, 3, TILE, HALF),
            vmem(CHUNKS, 3, 3, TILE, HALF),
            vmem(CHUNKS, 3, TILE, HALF),
            vmem(CHUNKS, 3, TILE, HALF),
            vmem(ROWS, 2, LON),
            vmem(2 * RING, 3, 2, HALF),
            vmem(CHUNKS, 3, TILE, HALF),
            vmem(CHUNKS, RING, 3, TILE, HALF),
            vmem(CHUNKS, ROWS, TILE, LON),
            vmem(CHUNKS, ROWS, TILE, LON),
            vmem(CHUNKS, ROWS, TILE, LON),
            vmem(CHUNKS, ROWS, TILE, LON),
            vmem(CHUNKS, ROWS, TILE, LON),
            vmem(ROWS, 2, LON),
            dma((CHUNKS, 2)),
            dma((CHUNKS, 2)),
            dma((3, CHUNKS)),
            dma((CHUNKS, 4)),
            dma((CHUNKS, 4)),
            dma((CHUNKS, 3)),
            dma((CHUNKS, 3)),
            dma((CHUNKS,)),
            dma((CHUNKS,)),
            dma((CHUNKS, 7)),
            dma((CHUNKS, 7)),
            dma((CHUNKS, 2)),
            dma((CHUNKS, 2)),
            dma((2 * RING,)),
            dma((2 * RING,)),
            dma((CHUNKS + 1,)),
        ],
        compiler_params=pltpu.CompilerParams(
            collective_id=0, has_side_effects=True, vmem_limit_bytes=60 * 1024 * 1024
        ),
        name="localize",
    )(
        half_width,
        control[0].transpose(1, 0, 2),
        perturbation[0].transpose(1, 0, 2),
        weight.transpose(1, 0, 2),
    )
    return increment.transpose(1, 0, 2), adjoint.transpose(1, 0, 2)[None]


def solution(mesh):
    return jax.shard_map(
        functools.partial(shards, mesh.shape["sub"]),
        mesh=mesh,
        in_specs=(
            P("grp", None, "sub", None),
            P("grp", None, "sub", None),
            P("grp", "sub", None),
            P(),
        ),
        out_specs=(P("grp", "sub", None), P("grp", None, "sub", None)),
        check_vma=False,
    )
```

time: 437 us -> 105 us (0.24)
  the two profiles are of different devices: /device:TPU:3 before, /device:TPU:1 now
where the time goes in v1:
time: 105 us
  Pallas kernels  100 us (95%)
  local copies, waits for them, and re-layouts  3.88 us (4%)
    pallas_call x1, Pallas kernels, shards(): pl.pallas_call(functools.partial(kernel, n_sub), out_shape=(jax.ShapeDtyp...  100 us
    unnamed x2, local copies, waits for them, and re-layouts  3.88 us

profile of v1, /device:TPU:1, one launch (start us, length us, event | category | flops | bytes accessed | tf_op | source)
XLA Modules:
  0.0 105.0 jit_solution(7942847912650679781)
XLA Ops:
  0.6 100.5 %localize.1 = (f32[12,2,768]{2,1,0:T(2,128)}, f32[12,32,768]{2,1,0:T(8,128)}) custom-call(s32[384]{0:T(512)} %hw.1, f32[12,32,768]{2,1,0:T(8,128)} %bitcast.12, f32[12,32,768]{2,1,0:T(8,128)} %bitcast.13, f32[12,2,768]{2,1,0:T(2,128)} %bitcast.14), custom_call_target="tpu_custom_call" | custom-call | tf_op jit(solution)/shard_map/localize/pallas_call | solution.py:379
  101.1 1.5 %copy.8 = f32[2,12,768]{2,0,1:T(2,128)} copy(f32[2,12,768]{2,0,1:T(2,128)} %bitcast.15) | data formatting | bytes 147456
  102.6 2.4 %copy.9 = f32[1,32,12,768]{3,1,2,0:T(8,128)} copy(f32[1,32,12,768]{3,1,2,0:T(8,128)} %bitcast.11) | data formatting | bytes 2359296

commit v2 on v1

v2 whole, which is shorter than its diff:
```python
import functools
import math

import jax
import jax.numpy as jnp
from jax import lax
from jax.experimental import pallas as pl
from jax.experimental.pallas import tpu as pltpu
from jax.sharding import PartitionSpec as P

MESH = pl.DeviceIdType.MESH
ROWS = 12
TILE = 8
CHUNKS = 4
LON = 768
HALF = 384
RING = 8
REACH = 12
LON_SUM = sum(math.exp(-0.5 * (d / 4.0) ** 2) for d in range(-REACH, REACH + 1))
WINDOW = 512
OUT = 256


def kernel(
    n_sub,
    hw,
    control,
    pert,
    weight,
    inc_out,
    adj_out,
    cbuf,
    pbuf,
    ybuf,
    lhs,
    lonw,
    wtab,
    prod,
    rsbuf,
    tot,
    xin,
    wpart,
    wbuf,
    wfull,
    inc,
    own,
    to_l,
    to_r,
    from_l,
    from_r,
    incst,
    c_send,
    c_recv,
    load_sem,
    rs_send,
    rs_recv,
    x_send,
    x_recv,
    ag_send,
    ag_recv,
    a_send,
    a_recv,
    w_send,
    w_recv,
    out_sem,
):
    g = lax.axis_index("grp")
    s = lax.axis_index("sub")
    y = lax.rem(g, RING)
    xh = lax.div(g, RING)
    base = xh * RING
    core = lax.rem(s, 2)
    sign = 1 - 2 * core
    left, has_left = jnp.maximum(s - 1, 0), s > 0
    right, has_right = jnp.minimum(s + 1, n_sub - 1), s < n_sub - 1

    def ring(offset):
        return lax.rem(y + sign * offset + RING, RING)

    partner = (1 - xh) * RING + y

    def remote(src, dst, ss, rs, grp, sub):
        return pltpu.make_async_remote_copy(
            src_ref=src, dst_ref=dst, send_sem=ss, recv_sem=rs, device_id=(grp, sub), device_id_type=MESH
        )

    pending = []

    def launch(copy):
        copy.start()
        pending.append(copy.wait_send)
        return copy

    class Halo:
        def __init__(self, copy, can_send, can_receive):
            self.copy, self.can_send, self.can_receive = copy, can_send, can_receive
            pl.when(can_send)(copy.start)
            pending.append(self.wait_send)

        def wait_send(self):
            pl.when(self.can_send)(self.copy.wait_send)

        def wait_recv(self):
            pl.when(self.can_receive)(self.copy.wait_recv)

    def exchange(for_right, at_left, for_left, at_right, ss, rs):
        return (
            Halo(remote(for_right, at_left, ss.at[0], rs.at[0], g, right), has_right, has_left),
            Halo(remote(for_left, at_right, ss.at[1], rs.at[1], g, left), has_left, has_right),
        )

    loads = {}
    for k in range(CHUNKS):
        levels = pl.ds(k * TILE, TILE)
        loads["c", k] = pltpu.make_async_copy(control.at[:, levels, :], cbuf.at[k, pl.ds(ROWS, ROWS)], load_sem.at[0, k])
        loads["p", k] = pltpu.make_async_copy(pert.at[:, levels, :], pbuf.at[k], load_sem.at[1, k])
        loads["c", k].start()
        loads["p", k].start()

    def weight_piece(ref, owner):
        rows = pl.ds(3 * lax.div(owner, 2), 3)
        cols = pl.ds(pl.multiple_of(lax.rem(owner, 2) * HALF, 128), HALF)
        return ref.at[rows, :, cols]

    loads["w"] = pltpu.make_async_copy(weight_piece(weight, y), wbuf.at[g], load_sem.at[2, 0])
    loads["w"].start()

    barrier = pltpu.get_barrier_semaphore()
    for grp, sub, there in ((g, left, has_left), (g, right, has_right)):
        @pl.when(there)
        def _(grp=grp, sub=sub):
            pl.semaphore_signal(barrier, inc=1, device_id=(grp, sub), device_id_type=MESH)

    for grp in (*(base + ring(j) for j in (1, -1, 2, -2)), partner):
        pl.semaphore_signal(barrier, inc=1, device_id=(grp, s), device_id_type=MESH)
    pl.semaphore_wait(barrier, 5 + has_left.astype(jnp.int32) + has_right.astype(jnp.int32))

    halos = {}

    def send_control(k):
        src = control.at[:, pl.ds(k * TILE, TILE), :]
        halos["c", k] = exchange(
            src, cbuf.at[k, pl.ds(0, ROWS)], src, cbuf.at[k, pl.ds(2 * ROWS, ROWS)], c_send.at[k], c_recv.at[k]
        )

    halos["w"] = launch(remote(weight, wpart, w_send.at[0], w_recv.at[0], partner, s))
    for k in range(CHUNKS):
        send_control(k)

    for there, at, incoming in ((has_left, 0, from_l), (has_right, 2 * ROWS, from_r)):
        @pl.when(jnp.logical_not(there))
        def _(at=at, incoming=incoming):
            def clear(k, carry):
                zero = jnp.zeros((TILE, LON), jnp.float32)
                for r in range(ROWS):
                    cbuf[k, at + r] = zero
                    incoming[k, r] = zero
                return carry

            lax.fori_loop(0, CHUNKS, clear, 0)

    def fill(r, carry):
        row = s * ROWS + r
        reach = jnp.full((8, 128), hw[row].astype(jnp.float32))
        spread = 0.5 * reach + 0.5
        inverse = 1.0 / spread
        at = jnp.full((8, 128), row)
        values = []
        total = jnp.ones((8, 128), jnp.float32)
        for d in range(ROWS + 1):
            e = jnp.where(d <= reach, jnp.exp(-0.5 * (d * inverse) ** 2), 0.0)
            values.append(e)
            if d:
                total = total + jnp.where(at - d >= 0, e, 0.0) + jnp.where(at + d < n_sub * ROWS, e, 0.0)
        scale = 1.0 / total
        for d in range(ROWS + 1):
            wtab[r, d] = values[d] * scale
        return carry

    lax.fori_loop(0, ROWS, fill, 0)

    def fill_lon(i, carry):
        start = pl.multiple_of(i * 64, 64)
        a = lax.broadcasted_iota(jnp.int32, (64, OUT), 0) + i * 64
        b = lax.broadcasted_iota(jnp.int32, (64, OUT), 1)
        d = (a - 128 - b).astype(jnp.float32)
        f = jnp.where(jnp.abs(d) <= REACH, jnp.exp(-0.5 * (d / 4.0) ** 2) / LON_SUM, 0.0)
        hi = f.astype(jnp.bfloat16)
        lonw[pl.ds(start, 64), :] = hi
        lonw[pl.ds(start + WINDOW, 64), :] = hi
        lonw[pl.ds(start + 2 * WINDOW, 64), :] = (f - hi.astype(jnp.float32)).astype(jnp.bfloat16)
        return carry

    lax.fori_loop(0, WINDOW // 64, fill_lon, 0)

    count = ROWS * TILE

    def lon_filter():
        for t in range(3):
            for i in range(4):
                c = (256 * t - 128 + 128 * i) % LON
                v = ybuf[:, c : c + 128]
                hi = v.astype(jnp.bfloat16)
                rows = slice(count * t, count * (t + 1))
                lhs[rows, 128 * i : 128 * (i + 1)] = hi
                lhs[rows, WINDOW + 128 * i : WINDOW + 128 * (i + 1)] = (v - hi.astype(jnp.float32)).astype(jnp.bfloat16)
                lhs[rows, 2 * WINDOW + 128 * i : 2 * WINDOW + 128 * (i + 1)] = hi
        for t in range(3):
            rows = slice(count * t, count * (t + 1))
            ybuf[:, OUT * t : OUT * (t + 1)] = jnp.dot(lhs[rows, :], lonw[...], preferred_element_type=jnp.float32)

    def piece_slices(o):
        return 3 * (o // 2), HALF * (o % 2)

    def forward(k):
        loads["c", k].wait()
        loads["p", k].wait()
        for copy in halos["c", k]:
            copy.wait_recv()

        def column(c, carry):
            lanes = pl.ds(pl.multiple_of(c * 128, 128), 128)
            x = [cbuf[k, i, :, lanes] for i in range(3 * ROWS)]
            for r in range(ROWS):
                acc = wtab[r, 0] * x[ROWS + r]
                for d in range(1, ROWS + 1):
                    acc = acc + wtab[r, d] * (x[ROWS + r - d] + x[ROWS + r + d])
                ybuf[r * TILE : (r + 1) * TILE, lanes] = acc
            return carry

        lax.fori_loop(0, LON // 128, column, 0)
        lon_filter()
        for o in range(RING):
            r0, c0 = piece_slices(o)
            part = ybuf[r0 * TILE : (r0 + 3) * TILE, c0 : c0 + HALF].reshape(3, TILE, HALF)
            prod[k, o] = part * pbuf[k, r0 : r0 + 3, :, c0 : c0 + HALF]

    reduce = {}

    def send_part(k, slot, src, hops):
        reduce[k, slot] = launch(
            remote(src, rsbuf.at[k, slot], rs_send.at[k, slot], rs_recv.at[k, slot], base + ring(hops), s)
        )

    def stage0(k):
        forward(k)
        for slot, (owner, hops) in enumerate(((4, 2), (3, 1), (-3, -1), (1, 1), (-1, -1))):
            send_part(k, slot, prod.at[k, ring(owner)], hops)

    def stage1(k):
        for slot in (0, 1, 2):
            reduce[k, slot].wait_recv()
        rsbuf[k, 0] = prod[k, ring(2)] + rsbuf[k, 0] + rsbuf[k, 1]
        send_part(k, 5, rsbuf.at[k, 0], 2)
        rsbuf[k, 2] = prod[k, ring(-2)] + rsbuf[k, 2]
        send_part(k, 6, rsbuf.at[k, 2], -2)

    def stage4(k):
        for slot in (3, 4, 5, 6):
            reduce[k, slot].wait_recv()
        tot[k] = prod[k, y] + rsbuf[k, 3] + rsbuf[k, 4] + rsbuf[k, 5] + rsbuf[k, 6]
        halos["x", k] = launch(remote(tot.at[k], xin.at[k], x_send.at[k], x_recv.at[k], partner, s))

    weights = []
    gather = {}

    def send_weights():
        halos["w"].wait_recv()
        for j in range(1, RING):
            dest = lax.rem(y + j, RING)
            for i, (ref, owner) in enumerate(((weight, g), (wpart, partner))):
                n = 2 * j + i
                weights.append(
                    launch(
                        remote(weight_piece(ref, dest), wbuf.at[owner], w_send.at[n], w_recv.at[n], base + dest, s)
                    )
                )
        loads["x"] = pltpu.make_async_copy(weight_piece(wpart, y), wbuf.at[partner], load_sem.at[2, 1])
        loads["x"].start()

    def take_weights():
        loads["w"].wait()
        loads["x"].wait()
        for copy in weights:
            copy.wait_recv()
        for i in range(2 * RING):
            wfull[i // 4, :, 2 * (i % 4) : 2 * (i % 4) + 2, :] = wbuf[i]

    def stage5(k):
        halos["x", k].wait_recv()
        inc[k, y] = wfull[k] * (tot[k] + xin[k])
        for slot, hops in enumerate((-2, 2, -1, 1)):
            send_inc(k, slot, y, hops)

    def send_inc(k, slot, owner, hops):
        piece = inc.at[k, owner]
        gather[k, slot] = launch(remote(piece, piece, ag_send.at[k, slot], ag_recv.at[k, slot], base + ring(hops), s))

    def stage6(k):
        gather[k, 0].wait_recv()
        send_inc(k, 4, ring(2), -2)
        send_inc(k, 5, ring(2), -1)
        gather[k, 1].wait_recv()
        send_inc(k, 6, ring(-2), 1)

    def stage8(k):
        for slot in (2, 3, 4, 5, 6):
            gather[k, slot].wait_recv()
        for o in range(RING):
            r0, c0 = piece_slices(o)
            p = inc[k, o] * pbuf[k, r0 : r0 + 3, :, c0 : c0 + HALF]
            ybuf[r0 * TILE : (r0 + 3) * TILE, c0 : c0 + HALF] = p.reshape(3 * TILE, HALF)
        lon_filter()

        def column(c, carry):
            lanes = pl.ds(pl.multiple_of(c * 128, 128), 128)
            acc = [None] * (3 * ROWS)
            for i in range(ROWS):
                p = ybuf[i * TILE : (i + 1) * TILE, lanes]
                for d in range(ROWS + 1):
                    term = wtab[i, d] * p
                    for j in {ROWS + i - d, ROWS + i + d}:
                        acc[j] = term if acc[j] is None else acc[j] + term
            for j in range(ROWS):
                to_l[k, j, :, lanes] = acc[j]
                own[k, j, :, lanes] = acc[ROWS + j]
                to_r[k, j, :, lanes] = acc[2 * ROWS + j]
            return carry

        lax.fori_loop(0, LON // 128, column, 0)
        halos["a", k] = exchange(to_r.at[k], from_l.at[k], to_l.at[k], from_r.at[k], a_send.at[k], a_recv.at[k])

    outs = []

    def stage7(k):
        for copy in halos["a", k]:
            copy.wait_recv()

        def row(r, carry):
            own[k, r] = own[k, r] + from_l[k, r] + from_r[k, r]
            return carry

        lax.fori_loop(0, ROWS, row, 0)
        copy = pltpu.make_async_copy(own.at[k], adj_out.at[:, pl.ds(k * TILE, TILE), :], out_sem.at[k])
        copy.start()
        outs.append(copy)

    def write_increment():
        chunk = lax.div(g, 4)
        j = jnp.full((3, 2, HALF), lax.rem(g, 4))
        for o in range(RING):
            r0, c0 = piece_slices(o)
            v = inc[chunk, o]
            part = v[:, 6:8]
            for i in (2, 1, 0):
                part = jnp.where(j == i, v[:, 2 * i : 2 * i + 2], part)
            incst[r0 : r0 + 3, :, c0 : c0 + HALF] = part
        copy = pltpu.make_async_copy(incst, inc_out, out_sem.at[CHUNKS])
        copy.start()
        outs.append(copy)

    events = []
    for k in range(CHUNKS):
        t = 3.1 * k
        events.append((t, functools.partial(stage0, k)))
        events.append((t + 4.0, functools.partial(stage1, k)))
        events.append((t + 8.0, functools.partial(stage4, k)))
        events.append((t + 11.7, functools.partial(stage5, k)))
        events.append((t + 15.2, functools.partial(stage6, k)))
        events.append((t + 18.7, functools.partial(stage8, k)))
        events.append((t + 30.0, functools.partial(stage7, k)))
    events.append((6.3, send_weights))
    events.append((11.6, take_weights))
    events.append((29.0, write_increment))
    for _, event in sorted(events, key=lambda e: e[0]):
        event()

    for wait_send in pending:
        wait_send()
    for copy in outs:
        copy.wait()


def finish(inc, adj, inc_out, adj_out, inc_tile, adj_tile, load_sem, store_sem):
    copies = []
    for k in range(CHUNKS):
        rows = pl.ds(3 * k, 3)
        copies.append(
            (
                pltpu.make_async_copy(adj.at[rows], adj_tile.at[rows], load_sem.at[k]),
                pltpu.make_async_copy(adj_tile.at[rows], adj_out.at[rows], store_sem.at[k]),
            )
        )
    copies.append(
        (
            pltpu.make_async_copy(inc, inc_tile, load_sem.at[CHUNKS]),
            pltpu.make_async_copy(inc_tile, inc_out, store_sem.at[CHUNKS]),
        )
    )
    for load, _ in copies:
        load.start()
    for load, store in copies:
        load.wait()
        store.start()
    for _, store in copies:
        store.wait()


def shards(n_sub, control, perturbation, weight, half_width):
    f32 = jnp.float32
    vmem = lambda *shape: pltpu.VMEM(shape, f32)
    dma = pltpu.SemaphoreType.DMA
    hbm = pl.BlockSpec(memory_space=pl.ANY)
    increment, adjoint = pl.pallas_call(
        functools.partial(kernel, n_sub),
        out_shape=(
            jax.ShapeDtypeStruct((ROWS, 2, LON), f32),
            jax.ShapeDtypeStruct((ROWS, CHUNKS * TILE, LON), f32),
        ),
        in_specs=[pl.BlockSpec(memory_space=pltpu.SMEM), hbm, hbm, hbm],
        out_specs=(hbm, hbm),
        scratch_shapes=[
            vmem(CHUNKS, 3 * ROWS, TILE, LON),
            vmem(CHUNKS, ROWS, TILE, LON),
            vmem(ROWS * TILE, LON),
            pltpu.VMEM((3 * ROWS * TILE, 3 * WINDOW), jnp.bfloat16),
            pltpu.VMEM((3 * WINDOW, OUT), jnp.bfloat16),
            vmem(ROWS, ROWS + 1, 8, 128),
            vmem(CHUNKS, RING, 3, TILE, HALF),
            vmem(CHUNKS, 7, 3, TILE, HALF),
            vmem(CHUNKS, 3, TILE, HALF),
            vmem(CHUNKS, 3, TILE, HALF),
            vmem(ROWS, 2, LON),
            vmem(2 * RING, 3, 2, HALF),
            vmem(CHUNKS, 3, TILE, HALF),
            vmem(CHUNKS, RING, 3, TILE, HALF),
            vmem(CHUNKS, ROWS, TILE, LON),
            vmem(CHUNKS, ROWS, TILE, LON),
            vmem(CHUNKS, ROWS, TILE, LON),
            vmem(CHUNKS, ROWS, TILE, LON),
            vmem(CHUNKS, ROWS, TILE, LON),
            vmem(ROWS, 2, LON),
            dma((CHUNKS, 2)),
            dma((CHUNKS, 2)),
            dma((3, CHUNKS)),
            dma((CHUNKS, 7)),
            dma((CHUNKS, 7)),
            dma((CHUNKS,)),
            dma((CHUNKS,)),
            dma((CHUNKS, 7)),
            dma((CHUNKS, 7)),
            dma((CHUNKS, 2)),
            dma((CHUNKS, 2)),
            dma((2 * RING,)),
            dma((2 * RING,)),
            dma((CHUNKS + 1,)),
        ],
        compiler_params=pltpu.CompilerParams(
            collective_id=0, has_side_effects=True, vmem_limit_bytes=60 * 1024 * 1024
        ),
        name="localize",
    )(
        half_width,
        control[0].transpose(1, 0, 2),
        perturbation[0].transpose(1, 0, 2),
        weight.transpose(1, 0, 2),
    )
    increment, adjoint = pl.pallas_call(
        finish,
        out_shape=(
            jax.ShapeDtypeStruct((ROWS, 2, LON), f32),
            jax.ShapeDtypeStruct((ROWS, CHUNKS * TILE, LON), f32),
        ),
        in_specs=[hbm, hbm],
        out_specs=(hbm, hbm),
        scratch_shapes=[
            vmem(ROWS, 2, LON),
            vmem(ROWS, CHUNKS * TILE, LON),
            dma((CHUNKS + 1,)),
            dma((CHUNKS + 1,)),
        ],
        name="finish",
    )(increment, adjoint)
    return increment.transpose(1, 0, 2), adjoint.transpose(1, 0, 2)[None]


def solution(mesh):
    return jax.shard_map(
        functools.partial(shards, mesh.shape["sub"]),
        mesh=mesh,
        in_specs=(
            P("grp", None, "sub", None),
            P("grp", None, "sub", None),
            P("grp", "sub", None),
            P(),
        ),
        out_specs=(P("grp", "sub", None), P("grp", None, "sub", None)),
        check_vma=False,
    )
```

time: 105 us -> 83 us (0.79)
  the two profiles are of different devices: /device:TPU:1 before, /device:TPU:385 now
where the time goes in v2:
time: 83 us; the launch traced here: 82.8 us
  Pallas kernels  82.2 us (99%)
    pallas_call x1, Pallas kernels, shards(): pl.pallas_call(functools.partial(kernel, n_sub), out_shape=(jax.ShapeDtyp...  80.1 us
    pallas_call x1, Pallas kernels, shards(): pl.pallas_call(finish, out_shape=(jax.ShapeDtypeStruct((ROWS, 2, LON), f3...  2.07 us

profile of v2, /device:TPU:385, one launch (start us, length us, event | category | flops | bytes accessed | tf_op | source)
XLA Modules:
  0.0 82.8 jit_solution(3993294221921348030)
XLA Ops:
  0.6 80.1 %localize.1 = (f32[12,2,768]{2,1,0:T(2,128)}, f32[12,32,768]{2,1,0:T(8,128)}) custom-call(s32[384]{0:T(512)} %hw.1, f32[12,32,768]{2,1,0:T(8,128)} %bitcast.11, f32[12,32,768]{2,1,0:T(8,128)} %bitcast.12, f32[12,2,768]{2,1,0:T(2,128)} %bitcast.13), custom_call_target="tpu_custom_call" | custom-call | tf_op jit(solution)/shard_map/localize/pallas_call | solution.py:414
  80.7 2.1 %finish.1 = (f32[12,2,768]{2,1,0:T(2,128)}, f32[12,32,768]{2,1,0:T(8,128)}) custom-call(f32[12,2,768]{2,1,0:T(2,128)} %get-tuple-element.6.inc, f32[12,32,768]{2,1,0:T(8,128)} %get-tuple-element.7.adj), custom_call_target="tpu_custom_call" | custom-call | tf_op jit(solution)/shard_map/finish/pallas_call | solution.py:468

commit v3 on v2

--- a/solution.py
+++ b/solution.py
@@ -69,13 +69,11 @@
     y = lax.rem(g, RING)
     xh = lax.div(g, RING)
     base = xh * RING
-    core = lax.rem(s, 2)
-    sign = 1 - 2 * core
     left, has_left = jnp.maximum(s - 1, 0), s > 0
     right, has_right = jnp.minimum(s + 1, n_sub - 1), s < n_sub - 1
 
     def ring(offset):
-        return lax.rem(y + sign * offset + RING, RING)
+        return lax.rem(y + offset + RING, RING)
 
     partner = (1 - xh) * RING + y
 
@@ -143,8 +141,9 @@
             src, cbuf.at[k, pl.ds(0, ROWS)], src, cbuf.at[k, pl.ds(2 * ROWS, ROWS)], c_send.at[k], c_recv.at[k]
         )
 
+    send_control(0)
     halos["w"] = launch(remote(weight, wpart, w_send.at[0], w_recv.at[0], partner, s))
-    for k in range(CHUNKS):
+    for k in range(1, CHUNKS):
         send_control(k)
 
     for there, at, incoming in ((has_left, 0, from_l), (has_right, 2 * ROWS, from_r)):
@@ -365,13 +364,13 @@
         events.append((t, functools.partial(stage0, k)))
         events.append((t + 4.0, functools.partial(stage1, k)))
         events.append((t + 8.0, functools.partial(stage4, k)))
-        events.append((t + 11.7, functools.partial(stage5, k)))
-        events.append((t + 15.2, functools.partial(stage6, k)))
-        events.append((t + 18.7, functools.partial(stage8, k)))
-        events.append((t + 30.0, functools.partial(stage7, k)))
-    events.append((6.3, send_weights))
-    events.append((11.6, take_weights))
-    events.append((29.0, write_increment))
+        events.append((t + 12.5, functools.partial(stage5, k)))
+        events.append((t + 16.5, functools.partial(stage6, k)))
+        events.append((t + 21.5, functools.partial(stage8, k)))
+        events.append((60.0 + k, functools.partial(stage7, k)))
+    events.append((8.1, send_weights))
+    events.append((12.4, take_weights))
+    events.append((59.0, write_increment))
     for _, event in sorted(events, key=lambda e: e[0]):
         event()
 

time: 83 us -> 80.9 us (0.975)
  the two profiles are of different devices: /device:TPU:385 before, /device:TPU:257 now
where the time goes in v3:
time: 80.9 us; the launch traced here: 80.8 us
  Pallas kernels  80.1 us (99%)
    pallas_call x1, Pallas kernels, shards(): pl.pallas_call(functools.partial(kernel, n_sub), out_shape=(jax.ShapeDtyp...  78.1 us
    pallas_call x1, Pallas kernels, shards(): pl.pallas_call(finish, out_shape=(jax.ShapeDtypeStruct((ROWS, 2, LON), f3...  2.07 us

profile of v3, /device:TPU:257, one launch (start us, length us, event | category | flops | bytes accessed | tf_op | source)
XLA Modules:
  0.0 80.8 jit_solution(3430166358713804590)
XLA Ops:
  0.6 78.1 %localize.1 = (f32[12,2,768]{2,1,0:T(2,128)}, f32[12,32,768]{2,1,0:T(8,128)}) custom-call(s32[384]{0:T(512)} %hw.1, f32[12,32,768]{2,1,0:T(8,128)} %bitcast.11, f32[12,32,768]{2,1,0:T(8,128)} %bitcast.12, f32[12,2,768]{2,1,0:T(2,128)} %bitcast.13), custom_call_target="tpu_custom_call" | custom-call | tf_op jit(solution)/shard_map/localize/pallas_call | solution.py:413
  78.7 2.1 %finish.1 = (f32[12,2,768]{2,1,0:T(2,128)}, f32[12,32,768]{2,1,0:T(8,128)}) custom-call(f32[12,2,768]{2,1,0:T(2,128)} %get-tuple-element.6.inc, f32[12,32,768]{2,1,0:T(8,128)} %get-tuple-element.7.adj), custom_call_target="tpu_custom_call" | custom-call | tf_op jit(solution)/shard_map/finish/pallas_call | solution.py:467

commit v4 on v3

--- a/solution.py
+++ b/solution.py
@@ -107,6 +107,14 @@
             Halo(remote(for_left, at_right, ss.at[1], rs.at[1], g, left), has_left, has_right),
         )
 
+    barrier = pltpu.get_barrier_semaphore()
+    for grp, sub, there in ((g, left, has_left), (g, right, has_right)):
+        @pl.when(there)
+        def _(grp=grp, sub=sub):
+            pl.semaphore_signal(barrier, inc=1, device_id=(grp, sub), device_id_type=MESH)
+
+    for grp in (*(base + ring(j) for j in (1, -1, 2, -2)), partner):
+        pl.semaphore_signal(barrier, inc=1, device_id=(grp, s), device_id_type=MESH)
     loads = {}
     for k in range(CHUNKS):
         levels = pl.ds(k * TILE, TILE)
@@ -123,14 +131,6 @@
     loads["w"] = pltpu.make_async_copy(weight_piece(weight, y), wbuf.at[g], load_sem.at[2, 0])
     loads["w"].start()
 
-    barrier = pltpu.get_barrier_semaphore()
-    for grp, sub, there in ((g, left, has_left), (g, right, has_right)):
-        @pl.when(there)
-        def _(grp=grp, sub=sub):
-            pl.semaphore_signal(barrier, inc=1, device_id=(grp, sub), device_id_type=MESH)
-
-    for grp in (*(base + ring(j) for j in (1, -1, 2, -2)), partner):
-        pl.semaphore_signal(barrier, inc=1, device_id=(grp, s), device_id_type=MESH)
     pl.semaphore_wait(barrier, 5 + has_left.astype(jnp.int32) + has_right.astype(jnp.int32))
 
     halos = {}
@@ -362,14 +362,14 @@
     for k in range(CHUNKS):
         t = 3.1 * k
         events.append((t, functools.partial(stage0, k)))
-        events.append((t + 4.0, functools.partial(stage1, k)))
-        events.append((t + 8.0, functools.partial(stage4, k)))
-        events.append((t + 12.5, functools.partial(stage5, k)))
-        events.append((t + 16.5, functools.partial(stage6, k)))
-        events.append((t + 21.5, functools.partial(stage8, k)))
+        events.append((t + 4.5, functools.partial(stage1, k)))
+        events.append((t + 9.0, functools.partial(stage4, k)))
+        events.append((t + 13.6, functools.partial(stage5, k)))
+        events.append((t + 18.0, functools.partial(stage6, k)))
+        events.append((t + 22.6, functools.partial(stage8, k)))
         events.append((60.0 + k, functools.partial(stage7, k)))
-    events.append((8.1, send_weights))
-    events.append((12.4, take_weights))
+    events.append((9.1, send_weights))
+    events.append((13.5, take_weights))
     events.append((59.0, write_increment))
     for _, event in sorted(events, key=lambda e: e[0]):
         event()

time: 80.9 us -> 80.9 us (level)
  no operation moved by 1% of the time
where the time goes in v4:
time: 80.9 us; the launch traced here: 80.7 us
  Pallas kernels  80.1 us (99%)
    pallas_call x1, Pallas kernels, shards(): pl.pallas_call(functools.partial(kernel, n_sub), out_shape=(jax.ShapeDtyp...  78 us
    pallas_call x1, Pallas kernels, shards(): pl.pallas_call(finish, out_shape=(jax.ShapeDtypeStruct((ROWS, 2, LON), f3...  2.07 us

profile of v4, /device:TPU:257, one launch (start us, length us, event | category | flops | bytes accessed | tf_op | source)
XLA Modules:
  0.0 80.7 jit_solution(2123599693278151326)
XLA Ops:
  0.6 78.0 %localize.1 = (f32[12,2,768]{2,1,0:T(2,128)}, f32[12,32,768]{2,1,0:T(8,128)}) custom-call(s32[384]{0:T(512)} %hw.1, f32[12,32,768]{2,1,0:T(8,128)} %bitcast.11, f32[12,32,768]{2,1,0:T(8,128)} %bitcast.12, f32[12,2,768]{2,1,0:T(2,128)} %bitcast.13), custom_call_target="tpu_custom_call" | custom-call | tf_op jit(solution)/shard_map/localize/pallas_call | solution.py:413
  78.7 2.1 %finish.1 = (f32[12,2,768]{2,1,0:T(2,128)}, f32[12,32,768]{2,1,0:T(8,128)}) custom-call(f32[12,2,768]{2,1,0:T(2,128)} %get-tuple-element.6.inc, f32[12,32,768]{2,1,0:T(8,128)} %get-tuple-element.7.adj), custom_call_target="tpu_custom_call" | custom-call | tf_op jit(solution)/shard_map/finish/pallas_call | solution.py:467
